TPU v7x, 128 devices: a whole 4x4x4 slice. The times are simulated.
128 devices in a mesh: outer: 8 (over z, core), inner: 16 (over x, y).
Axes of the slice: x: 4, y: 4, z: 4, core: 2. Of those that a mesh axis runs over, the one named last changes fastest.
Arguments:
- queries: bfloat16 [131072, 2048], P(('outer', 'inner')), may hold values from -6 to 6
- key_rows: bfloat16 [131072, 2048], P(('outer', 'inner')), may hold values from -6 to 6
- value_rows: bfloat16 [131072, 2048], P(('outer', 'inner')), may hold values from -6 to 6
- norm_gain: float32 [2048], replicated, may hold values from 0.5 to 1.5
Outputs:
- mixed: bfloat16 [131072, 2048], P(('outer', 'inner'))
- final_state: float32 [131072], P(('outer', 'inner'))
All inputs are finite; a program needn't handle non-finite values.
Results may differ from a plain program's by a relative error of at most 0.005.
Values sent between devices are 32-bit elements; how exact they have to be, the bound alone decides.
No kernel may reach another device: no remote copies, remote signals or barrier semaphores. Data moves between devices by JAX's collectives and lax.ppermute only.
A program may use at most 256 MiB of HBM per device.

v0:
```python
import jax
import jax.numpy as jnp
from jax import lax
from jax.sharding import PartitionSpec as P

D = 2048
HEADS = 32
DK = 64
BLOCK = 128


def carried_in(array, axis, combine, identity):
    length, here = (lax.axis_size(axis), lax.axis_index(axis))
    everything = lax.all_gather(array, axis)
    start = jnp.broadcast_to(jnp.asarray(identity, array.dtype), array.shape)

    def turn(k, before):
        reached = k < here
        new = combine(before, everything[k])
        return jnp.where(reached, new, before)

    return lax.fori_loop(0, length, turn, start)


def from_root(array, axis, root):
    mine = lax.axis_index(axis) == root
    return lax.psum(jnp.where(mine, array, jnp.zeros_like(array)), axis)


def combine_add(earlier, later):
    return earlier + later


def shards(queries, key_rows, value_rows, norm_gain):
    local_rows = queries.shape[0]
    blocks = local_rows // BLOCK
    query_grid = queries.reshape(blocks, BLOCK, HEADS, DK)
    key_grid = key_rows.reshape(blocks, BLOCK, HEADS, DK)
    value_grid = value_rows.reshape(blocks, BLOCK, HEADS, DK)
    block_states = jnp.einsum(
        "nkhd,nkhe->nhde", key_grid, value_grid, preferred_element_type=jnp.float32
    )
    later_index = lax.broadcasted_iota(jnp.int32, (blocks, blocks), 0)
    earlier_index = lax.broadcasted_iota(jnp.int32, (blocks, blocks), 1)
    lower = (earlier_index < later_index).astype(jnp.float32)
    flat_states = block_states.reshape(blocks, HEADS * DK * DK)
    before_block = jnp.dot(
        lower, flat_states, precision=lax.Precision.HIGHEST, preferred_element_type=jnp.float32
    ).reshape(blocks, HEADS, DK, DK)
    own_total = jnp.sum(flat_states, axis=0).reshape(HEADS, DK * DK)
    zero_state = jnp.zeros_like(own_total)
    causal = jnp.tril(jnp.ones((BLOCK, BLOCK), jnp.float32))
    scores = (
        jnp.einsum("nqhd,nkhd->nhqk", query_grid, key_grid, preferred_element_type=jnp.float32)
        * causal
    )
    weights = scores.astype(jnp.bfloat16)
    inside = jnp.einsum("nhqk,nkhe->nqhe", weights, value_grid, preferred_element_type=jnp.float32)
    prefix = carried_in(own_total, ("outer", "inner"), combine_add, zero_state)
    devices = lax.axis_size("outer") * lax.axis_size("inner")
    share = HEADS * DK * DK // devices
    scale_total = float(local_rows * devices) ** (-0.5)
    last_state = from_root(
        (prefix + own_total).reshape(HEADS * DK * DK), ("outer", "inner"), devices - 1
    )
    rank = lax.axis_index("outer") * lax.axis_size("inner") + lax.axis_index("inner")
    own_share = lax.dynamic_slice_in_dim(last_state, rank * share, share, 0)
    final_state = own_share * scale_total
    states = (prefix.reshape(1, HEADS, DK, DK) + before_block).astype(jnp.bfloat16)
    carried = jnp.einsum("nqhd,nhde->nqhe", query_grid, states, preferred_element_type=jnp.float32)
    attended = carried + inside
    gain_grid = norm_gain.reshape(HEADS, DK)
    scaled = (
        attended
        * lax.rsqrt(jnp.mean(attended * attended, axis=-1, keepdims=True) + 1e-06)
        * gain_grid
    )
    mixed = scaled.reshape(local_rows, D).astype(jnp.bfloat16)
    return (mixed, final_state)


def solution(mesh):
    return jax.shard_map(
        shards,
        mesh=mesh,
        in_specs=(
            P(("outer", "inner"), None),
            P(("outer", "inner"), None),
            P(("outer", "inner"), None),
            P(),
        ),
        out_specs=(P(("outer", "inner"), None), P(("outer", "inner"))),
        check_vma=False,
    )
```

profile of v0, /device:TPU:1, one launch (start us, length us, event | category | flops | bytes accessed | tf_op | source)
XLA Modules:
  0.0 548.3 jit_solution(6453652981230500022)
XLA Ops:
  7.2 12.9 %reshape.56 = bf16[8,128,32,64]{3,2,1,0:T(8,128)(2,1)} reshape(bf16[1024,2048]{1,0:T(8,128)(2,1)} %param.7) | data formatting | bytes 8388608 | tf_op jit(solution)/shard_map/reshape | solution.py:38
  20.1 11.5 %copy.35 = bf16[8,128,32,64]{1,3,2,0:T(8,128)(2,1)} copy(bf16[8,128,32,64]{3,2,1,0:T(8,128)(2,1)} %reshape.56) | data formatting | bytes 8388608 | tf_op jit(solution)/shard_map/reshape | solution.py:38
  31.6 12.9 %reshape.57 = bf16[8,128,32,64]{3,2,1,0:T(8,128)(2,1)} reshape(bf16[1024,2048]{1,0:T(8,128)(2,1)} %param.8) | data formatting | bytes 8388608 | tf_op jit(solution)/shard_map/reshape | solution.py:39
  44.4 11.5 %copy.36 = bf16[8,128,32,64]{1,3,2,0:T(8,128)(2,1)} copy(bf16[8,128,32,64]{3,2,1,0:T(8,128)(2,1)} %reshape.57) | data formatting | bytes 8388608 | tf_op jit(solution)/shard_map/reshape | solution.py:39
  55.9 9.0 %fusion.10 = (f32[32,64,64]{2,1,0:T(8,128)S(1)}, f32[8,32,64,64]{3,2,1,0:T(8,128)}) fusion(bf16[8,128,32,64]{1,3,2,0:T(8,128)(2,1)} %copy.35, bf16[8,128,32,64]{1,3,2,0:T(8,128)(2,1)} %copy.36), kind=kOutput, calls=%fused_computation.18 | convolution fusion | flops 269352960 | bytes 13107200 | tf_op jit(solution)/shard_map/nkhd,nkhe->nhde/dot_general | solution.py:40
  66.9 12.9 %reshape.58 = bf16[8,128,32,64]{3,2,1,0:T(8,128)(2,1)} reshape(bf16[1024,2048]{1,0:T(8,128)(2,1)} %param.6) | data formatting | bytes 8388608 | tf_op jit(solution)/shard_map/reshape | solution.py:37
  79.7 11.6 %copy.40 = bf16[8,128,32,64]{1,3,2,0:T(8,128)(2,1)} copy(bf16[8,128,32,64]{3,2,1,0:T(8,128)(2,1)} %reshape.58) | data formatting | bytes 8388608 | tf_op jit(solution)/shard_map/reshape | solution.py:37
  91.3 7.7 %reshape.51 = f32[8,131072]{1,0:T(8,128)} reshape(f32[8,32,64,64]{3,2,1,0:T(8,128)} %get-tuple-element.112) | data formatting | bytes 8388608 | tf_op jit(solution)/shard_map/reshape | solution.py:46
  99.0 8.7 %dot_general.21 = f32[32,64,64,8]{2,1,0,3:T(8,128)} reshape(f32[131072,8]{0,1:T(8,128)} %bitcast.37) | data formatting | bytes 8388608 | tf_op jit(solution)/shard_map/dot_general | solution.py:47
  107.7 126.6 %all-gather.2.cloned.1.call-done = f32[128,32,4096]{2,1,0:T(8,128)} async-done(((f32[1,32,4096]{2,1,0:T(8,128)}), f32[128,32,4096]{2,1,0:T(8,128)}) %all-gather.2.cloned.1.call-update) | async-done | bytes 67108880 | tf_op jit(solution)/shard_map/all_gather | solution.py:14
  234.3 158.9 %while.14 = (s32[]{:T(128)}, f32[32,4096]{1,0:T(8,128)S(1)}, s32[]{:T(128)}, f32[128,32,4096]{2,1,0:T(8,128)}, s32[]{:T(128)}, /*index=5*/s32[]{:T(128)}) while((s32[]{:T(128)}, f32[32,4096]{1,0:T(8,128)S(1)}, s32[]{:T(128)}, f32[128,32,4096]{2,1,0:T(8,128)}, s32[]{:T(128)}, /*index=5*/s32[]{:T(128)}) %tuple.41), condition=%wide.region_2.3_spmd.clone, body=%wide.region_1.2_spmd.clone.sunk | while | flops 393220 | bytes 1572965 | solution.py:22
  235.6 1.2 add_select_fusion.2
  236.8 1.2 add_select_fusion.2
  238.1 1.2 add_select_fusion.2
  239.3 1.2 add_select_fusion.2
  240.5 1.2 add_select_fusion.2
  241.8 1.2 add_select_fusion.2
  243.0 1.2 add_select_fusion.2
  244.3 1.2 add_select_fusion.2
  245.5 1.2 add_select_fusion.2
  246.7 1.2 add_select_fusion.2
  248.0 1.2 add_select_fusion.2
  249.2 1.2 add_select_fusion.2
  250.5 1.2 add_select_fusion.2
  251.7 1.2 add_select_fusion.2
  252.9 1.2 add_select_fusion.2
  254.2 1.2 add_select_fusion.2
  255.4 1.2 add_select_fusion.2
  256.7 1.2 add_select_fusion.2
  257.9 1.2 add_select_fusion.2
  259.1 1.2 add_select_fusion.2
  260.4 1.2 add_select_fusion.2
  261.6 1.2 add_select_fusion.2
  262.9 1.2 add_select_fusion.2
  264.1 1.2 add_select_fusion.2
  265.3 1.2 add_select_fusion.2
  266.6 1.2 add_select_fusion.2
  267.8 1.2 add_select_fusion.2
  269.1 1.2 add_select_fusion.2
  270.3 1.2 add_select_fusion.2
  271.5 1.2 add_select_fusion.2
  272.8 1.2 add_select_fusion.2
  274.0 1.2 add_select_fusion.2
  275.3 1.2 add_select_fusion.2
  276.5 1.2 add_select_fusion.2
  277.7 1.2 add_select_fusion.2
  279.0 1.2 add_select_fusion.2
  280.2 1.2 add_select_fusion.2
  281.5 1.2 add_select_fusion.2
  282.7 1.2 add_select_fusion.2
  283.9 1.2 add_select_fusion.2
  285.2 1.2 add_select_fusion.2
  286.4 1.2 add_select_fusion.2
  287.7 1.2 add_select_fusion.2
  288.9 1.2 add_select_fusion.2
  290.1 1.2 add_select_fusion.2
  394.7 12.6 %add_convert_fusion = bf16[8,32,64,64]{3,0,2,1:T(8,128)(2,1)S(1)} fusion(f32[32,64,64]{2,1,0:T(8,128)S(1)} %add.66, f32[32,64,64,8]{2,1,0,3:T(8,128)} %dot_general.21), kind=kOutput, calls=%fused_computation.7 | convolution fusion | flops 102760512 | bytes 6815744 | tf_op jit(solution)/shard_map/dot_general | solution.py:47
  407.4 4.8 fusion.2
  412.1 14.9 %multiply_reduce_fusion = (f32[8,128,32]{1,2,0:T(8,128)S(1)}, f32[8,32,128,64]{2,3,1,0:T(8,128)}) fusion(f32[8,32,64,128]{3,2,1,0:T(8,128)} %fusion.2, bf16[8,128,32,64]{1,3,2,0:T(8,128)(2,1)} %copy.36, bf16[8,128,32,64]{1,3,2,0:T(8,128)(2,1)} %copy.40, bf16[8,128,32,64]{1,3,2,0:T(8,128)(2,1)} %copy.35, f32[128,128]{1,0:T(8,128)S(1)} %fusion.7), kind=kOutput, calls=%fused_computation.6 | convolution fusion | flops 1088389120 | bytes 29556736 | tf_op jit(solution)/shard_map/nhqk,nkhe->nqhe/dot_general | solution.py:58
  427.0 8.6 %multiply_convert_fusion.1 = bf16[8,128,32,64]{1,3,2,0:T(8,128)(2,1)} fusion(f32[32,64]{1,0:T(8,128)S(1)} %mul.49, f32[8,128,32]{1,2,0:T(8,128)S(1)} %add_rsqrt_fusion, f32[8,32,128,64]{2,3,1,0:T(8,128)} %get-tuple-element.114, f32[8,32,64,128]{3,2,1,0:T(8,128)} %fusion.2), kind=kLoop, calls=%fused_computation.5 | loop fusion | flops 8388608 | bytes 21110784 | tf_op jit(solution)/shard_map/convert_element_type | solution.py:78
  435.6 12.8 %copy.47 = bf16[8,128,32,64]{3,2,1,0:T(8,128)(2,1)} copy(bf16[8,128,32,64]{1,3,2,0:T(8,128)(2,1)} %multiply_convert_fusion.1) | data formatting | bytes 8388608
  448.4 12.3 %reshape.55 = bf16[1024,2048]{1,0:T(8,128)(2,1)} reshape(bf16[8,128,32,64]{3,2,1,0:T(8,128)(2,1)} %copy.47) | data formatting | bytes 8388608
  460.7 79.4 %all-reduce.2.cloned.1.call-done = f32[131072]{0:T(1024)} async-done(((f32[131072]{0:T(1024)}), f32[131072]{0:T(1024)}) %all-reduce.2.cloned.1.call-update) | async-done | bytes 524304 | tf_op jit(solution)/shard_map/psum | solution.py:27
  540.1 1.3 dynamic-slice_multiply_fusion
  (100 shorter events, 104.3 us)
Async XLA Ops:
  7.2 227.2 %all-gather.2.cloned.1.call-start = ((), (), s32[]{:S(2)}) async-start(), calls=%async_computation | async-start | bytes 67633152 | tf_op jit(solution)/shard_map/all_gather | solution.py:14
  55.9 10.8 %copy-start.1 = (f32[2048]{0:T(1024)S(1)}, f32[2048]{0:T(1024)}, u32[]{:S(2)}) copy-start(f32[2048]{0:T(1024)} %param.9) | copy-start | bytes 24580
  66.2 474.0 %all-reduce.2.cloned.1.call-start = ((), (), s32[]{:S(2)}) async-start(), calls=%async_computation.1 | async-start | bytes 1048576 | tf_op jit(solution)/shard_map/psum | solution.py:27
  394.7 12.6 %copy-start = (bf16[8,128,32,64]{1,3,2,0:T(8,128)(2,1)S(1)}, bf16[8,128,32,64]{1,3,2,0:T(8,128)(2,1)}, u32[]{:S(2)}) copy-start(bf16[8,128,32,64]{1,3,2,0:T(8,128)(2,1)} %copy.40) | copy-start | bytes 12582916
Sparse Core Ops, SparseCore 0:
  66.3 168.0 all-gather.1
  394.8 145.2 all-reduce.1
where the time goes:
time: 557 us; the launch traced here: 548 us
  waiting for transfers between devices  206 us (37%)
  other arithmetic  166 us (30%)
  local copies, waits for them, and re-layouts  118 us (21%)
  matrix products  41.3 us (7%)
  between operations  14.1 us (3%)
    select_n x128, other arithmetic, turn(): return jnp.where(reached, new, before)  156 us
    all_gather x1, waiting for transfers between devices, carried_in(): everything = lax.all_gather(array, axis)  127 us
    psum x1, waiting for transfers between devices, from_root(): return lax.psum(jnp.where(mine, array, jnp.zeros_like(array)), axis)  79.4 us
    unnamed x7, local copies, waits for them, and re-layouts  26.1 us
    reshape x2, local copies, waits for them, and re-layouts, shards(): query_grid = queries.reshape(blocks, BLOCK, HEADS, DK)  24.5 us
    reshape x2, local copies, waits for them, and re-layouts, shards(): value_grid = value_rows.reshape(blocks, BLOCK, HEADS, DK)  24.4 us
    reshape x2, local copies, waits for them, and re-layouts, shards(): key_grid = key_rows.reshape(blocks, BLOCK, HEADS, DK)  24.3 us
    dot_general x1, matrix products, shards(): jnp.einsum('nhqk,nkhe->nqhe', weights, value_grid, preferred_element_type...  14.9 us
  transfers between devices with their start and end apart: 2, of which 2 were waited for; matrix products, arithmetic and copies ran while one was open for 20% of the time, Pallas kernels for 0%

commit v1 on v0

--- a/solution.py
+++ b/solution.py
@@ -24,7 +24,7 @@
 
 def from_root(array, axis, root):
     mine = lax.axis_index(axis) == root
-    return lax.psum(jnp.where(mine, array, jnp.zeros_like(array)), axis)
+    return jnp.sum(lax.all_gather(jnp.where(mine, array, jnp.zeros_like(array)), axis), axis=0)
 
 
 def combine_add(earlier, later):

time: 557 us -> 621 us (1.11)
  other arithmetic: 166 us -> 214 us
  waiting for transfers between devices: 206 us -> 221 us
    psum x1 -> x0, waiting for transfers between devices: 79.4 us -> none  [from_root(): return lax.psum(jnp.where(mine, array, jnp.zeros_like(array)), axis)]
    all_gather x0 -> x1, waiting for transfers between devices: none -> 53.5 us  [from_root(): lax.all_gather(jnp.where(mine, array, jnp.zeros_like(array)), axis)]
    reduce_sum x0 -> x1, other arithmetic: none -> 46.7 us  [from_root(): jnp.sum(lax.all_gather(jnp.where(mine, array, jnp.zeros_like(array)), axi...]
    all_gather x1, waiting for transfers between devices: 127 us -> 168 us  [carried_in(): everything = lax.all_gather(array, axis)]
  transfers between devices with their start and end apart: 2 -> 2, of which waited for: 2 -> 2; matrix products, arithmetic and copies ran while one was open for 20% -> 18% of each run, Pallas kernels for 0% -> 0%
where the time goes in v1:
time: 621 us; the launch traced here: 612 us
  waiting for transfers between devices  221 us (36%)
  other arithmetic  214 us (34%)
  local copies, waits for them, and re-layouts  119 us (19%)
  matrix products  41.4 us (7%)
  between operations  14.1 us (2%)
    all_gather x1, waiting for transfers between devices, carried_in(): everything = lax.all_gather(array, axis)  168 us
    select_n x128, other arithmetic, turn(): return jnp.where(reached, new, before)  156 us
    all_gather x1, waiting for transfers between devices, from_root(): lax.all_gather(jnp.where(mine, array, jnp.zeros_like(array)), axis)  53.5 us
    reduce_sum x1, other arithmetic, from_root(): jnp.sum(lax.all_gather(jnp.where(mine, array, jnp.zeros_like(array)), axi...  46.7 us
    unnamed x7, local copies, waits for them, and re-layouts  27.2 us
    reshape x2, local copies, waits for them, and re-layouts, shards(): query_grid = queries.reshape(blocks, BLOCK, HEADS, DK)  24.4 us
    reshape x2, local copies, waits for them, and re-layouts, shards(): value_grid = value_rows.reshape(blocks, BLOCK, HEADS, DK)  24.4 us
    reshape x2, local copies, waits for them, and re-layouts, shards(): key_grid = key_rows.reshape(blocks, BLOCK, HEADS, DK)  24.3 us
  transfers between devices with their start and end apart: 2, of which 2 were waited for; matrix products, arithmetic and copies ran while one was open for 18% of the time, Pallas kernels for 0%

profile of v1, /device:TPU:1, one launch (start us, length us, event | category | flops | bytes accessed | tf_op | source)
XLA Modules:
  0.0 612.3 jit_solution(9863920961940308960)
XLA Ops:
  7.2 12.9 %reshape.69 = bf16[8,128,32,64]{3,2,1,0:T(8,128)(2,1)} reshape(bf16[1024,2048]{1,0:T(8,128)(2,1)} %param.7) | data formatting | bytes 8388608 | tf_op jit(solution)/shard_map/reshape | solution.py:38
  20.1 11.5 %copy.35 = bf16[8,128,32,64]{1,3,2,0:T(8,128)(2,1)} copy(bf16[8,128,32,64]{3,2,1,0:T(8,128)(2,1)} %reshape.69) | data formatting | bytes 8388608 | tf_op jit(solution)/shard_map/reshape | solution.py:38
  31.6 12.9 %reshape.70 = bf16[8,128,32,64]{3,2,1,0:T(8,128)(2,1)} reshape(bf16[1024,2048]{1,0:T(8,128)(2,1)} %param.8) | data formatting | bytes 8388608 | tf_op jit(solution)/shard_map/reshape | solution.py:39
  44.4 11.5 %copy.36 = bf16[8,128,32,64]{1,3,2,0:T(8,128)(2,1)} copy(bf16[8,128,32,64]{3,2,1,0:T(8,128)(2,1)} %reshape.70) | data formatting | bytes 8388608 | tf_op jit(solution)/shard_map/reshape | solution.py:39
  55.9 9.0 %fusion.10 = (f32[32,64,64]{2,1,0:T(8,128)S(1)}, f32[8,32,64,64]{3,2,1,0:T(8,128)}) fusion(bf16[8,128,32,64]{1,3,2,0:T(8,128)(2,1)} %copy.35, bf16[8,128,32,64]{1,3,2,0:T(8,128)(2,1)} %copy.36), kind=kOutput, calls=%fused_computation.18 | convolution fusion | flops 269352960 | bytes 13107200 | tf_op jit(solution)/shard_map/nkhd,nkhe->nhde/dot_general | solution.py:40
  66.6 167.7 %all-gather.4.cloned.1.call-done = f32[128,32,4096]{2,1,0:T(8,128)} async-done(((f32[1,32,4096]{2,1,0:T(8,128)}), f32[128,32,4096]{2,1,0:T(8,128)}) %all-gather.4.cloned.1.call-update) | async-done | bytes 67108880 | tf_op jit(solution)/shard_map/all_gather | solution.py:14
  234.3 158.7 %while.14 = (s32[]{:T(128)}, f32[32,4096]{1,0:T(8,128)S(1)}, s32[]{:T(128)}, f32[128,32,4096]{2,1,0:T(8,128)}, s32[]{:T(128)}, /*index=5*/s32[]{:T(128)}) while((s32[]{:T(128)}, f32[32,4096]{1,0:T(8,128)S(1)}, s32[]{:T(128)}, f32[128,32,4096]{2,1,0:T(8,128)}, s32[]{:T(128)}, /*index=5*/s32[]{:T(128)}) %tuple.41), condition=%wide.region_2.3_spmd.clone, body=%wide.region_1.2_spmd.clone.sunk | while | flops 393220 | bytes 1572965 | solution.py:22
  235.5 1.2 add_select_fusion.3
  236.8 1.2 add_select_fusion.3
  238.0 1.2 add_select_fusion.3
  239.3 1.2 add_select_fusion.3
  240.5 1.2 add_select_fusion.3
  241.7 1.2 add_select_fusion.3
  243.0 1.2 add_select_fusion.3
  244.2 1.2 add_select_fusion.3
  245.5 1.2 add_select_fusion.3
  246.7 1.2 add_select_fusion.3
  247.9 1.2 add_select_fusion.3
  249.2 1.2 add_select_fusion.3
  250.4 1.2 add_select_fusion.3
  251.7 1.2 add_select_fusion.3
  252.9 1.2 add_select_fusion.3
  254.1 1.2 add_select_fusion.3
  255.4 1.2 add_select_fusion.3
  256.6 1.2 add_select_fusion.3
  257.9 1.2 add_select_fusion.3
  259.1 1.2 add_select_fusion.3
  260.3 1.2 add_select_fusion.3
  261.6 1.2 add_select_fusion.3
  262.8 1.2 add_select_fusion.3
  264.1 1.2 add_select_fusion.3
  265.3 1.2 add_select_fusion.3
  266.5 1.2 add_select_fusion.3
  267.8 1.2 add_select_fusion.3
  269.0 1.2 add_select_fusion.3
  270.3 1.2 add_select_fusion.3
  271.5 1.2 add_select_fusion.3
  272.7 1.2 add_select_fusion.3
  274.0 1.2 add_select_fusion.3
  275.2 1.2 add_select_fusion.3
  276.5 1.2 add_select_fusion.3
  277.7 1.2 add_select_fusion.3
  278.9 1.2 add_select_fusion.3
  280.2 1.2 add_select_fusion.3
  281.4 1.2 add_select_fusion.3
  282.7 1.2 add_select_fusion.3
  283.9 1.2 add_select_fusion.3
  285.1 1.2 add_select_fusion.3
  286.4 1.2 add_select_fusion.3
  287.6 1.2 add_select_fusion.3
  288.9 1.2 add_select_fusion.3
  393.1 1.4 reshape.64
  394.6 12.9 %reshape.71 = bf16[8,128,32,64]{3,2,1,0:T(8,128)(2,1)} reshape(bf16[1024,2048]{1,0:T(8,128)(2,1)} %param.6) | data formatting | bytes 8388608 | tf_op jit(solution)/shard_map/reshape | solution.py:37
  407.6 11.5 %copy.40 = bf16[8,128,32,64]{1,3,2,0:T(8,128)(2,1)} copy(bf16[8,128,32,64]{3,2,1,0:T(8,128)(2,1)} %reshape.71) | data formatting | bytes 8388608 | tf_op jit(solution)/shard_map/reshape | solution.py:37
  419.1 7.8 %reshape.61 = f32[8,131072]{1,0:T(8,128)} reshape(f32[8,32,64,64]{3,2,1,0:T(8,128)} %get-tuple-element.112) | data formatting | bytes 8388608 | tf_op jit(solution)/shard_map/reshape | solution.py:46
  426.9 8.7 %dot_general.21 = f32[32,64,64,8]{2,1,0,3:T(8,128)} reshape(f32[131072,8]{0,1:T(8,128)} %bitcast.34) | data formatting | bytes 8388608 | tf_op jit(solution)/shard_map/dot_general | solution.py:47
  436.0 13.0 %add_convert_fusion = bf16[8,32,64,64]{3,0,2,1:T(8,128)(2,1)S(1)} fusion(f32[32,64,64]{2,1,0:T(8,128)S(1)} %add.64, f32[32,64,64,8]{2,1,0,3:T(8,128)} %dot_general.21), kind=kOutput, calls=%fused_computation.7 | convolution fusion | flops 102760512 | bytes 6815744 | tf_op jit(solution)/shard_map/dot_general | solution.py:47
  449.0 4.7 fusion.2
  453.7 14.6 %multiply_reduce_fusion = (f32[8,128,32]{1,2,0:T(8,128)S(1)}, f32[8,32,128,64]{2,3,1,0:T(8,128)}) fusion(f32[8,32,64,128]{3,2,1,0:T(8,128)} %fusion.2, bf16[8,128,32,64]{1,3,2,0:T(8,128)(2,1)} %copy.36, bf16[8,128,32,64]{1,3,2,0:T(8,128)(2,1)} %copy.40, bf16[8,128,32,64]{1,3,2,0:T(8,128)(2,1)} %copy.35, f32[128,128]{1,0:T(8,128)S(1)} %fusion.7), kind=kOutput, calls=%fused_computation.6 | convolution fusion | flops 1088389120 | bytes 29556736 | tf_op jit(solution)/shard_map/nhqk,nkhe->nqhe/dot_general | solution.py:58
  468.4 10.5 %multiply_convert_fusion.1 = bf16[8,128,32,64]{1,3,2,0:T(8,128)(2,1)} fusion(f32[32,64]{1,0:T(8,128)S(1)} %mul.49, f32[8,128,32]{1,2,0:T(8,128)S(1)} %add_rsqrt_fusion, f32[8,32,128,64]{2,3,1,0:T(8,128)} %get-tuple-element.114, f32[8,32,64,128]{3,2,1,0:T(8,128)} %fusion.2), kind=kLoop, calls=%fused_computation.5 | loop fusion | flops 8388608 | bytes 21110784 | tf_op jit(solution)/shard_map/convert_element_type | solution.py:78
  478.9 13.1 %copy.47 = bf16[8,128,32,64]{3,2,1,0:T(8,128)(2,1)} copy(bf16[8,128,32,64]{1,3,2,0:T(8,128)(2,1)} %multiply_convert_fusion.1) | data formatting | bytes 8388608
  492.0 12.7 %reshape.68 = bf16[1024,2048]{1,0:T(8,128)(2,1)} reshape(bf16[8,128,32,64]{3,2,1,0:T(8,128)(2,1)} %copy.47) | data formatting | bytes 8388608
  504.7 53.5 %all-gather.6.cloned.1.call-done = f32[128,1,131072]{2,1,0:T(1,128)} async-done(((f32[1,1,131072]{2,1,0:T(1,128)}), f32[128,1,131072]{2,1,0:T(1,128)}) %all-gather.6.cloned.1.call-update) | async-done | bytes 67108880 | tf_op jit(solution)/shard_map/all_gather | solution.py:27
  558.2 46.7 %reduce_sum.29 = f32[131072]{0:T(1024)S(1)} reduce(f32[128,1,131072]{2,1,0:T(1,128)} %all-gather.6.cloned.1.call-done, f32[]{:T(128)} %constant.44.clone.1), dimensions={0,1}, to_apply=%region_4.5 | reduce | flops 16646144 | bytes 67633152 | tf_op jit(solution)/shard_map/reduce_sum | solution.py:27
  (101 shorter events, 105.0 us)
Async XLA Ops:
  7.2 227.1 %all-gather.4.cloned.1.call-start = ((), (), s32[]{:S(2)}) async-start(), calls=%async_computation | async-start | bytes 67633152 | tf_op jit(solution)/shard_map/all_gather | solution.py:14
  65.0 329.6 %copy-start.1 = (f32[2048]{0:T(1024)S(1)}, f32[2048]{0:T(1024)}, u32[]{:S(2)}) copy-start(f32[2048]{0:T(1024)} %param.9) | copy-start | bytes 24580
  66.1 492.1 %all-gather.6.cloned.1.call-start = ((), (), s32[]{:S(2)}) async-start(), calls=%async_computation.1 | async-start | bytes 67633152 | tf_op jit(solution)/shard_map/all_gather | solution.py:27
  436.0 13.0 %copy-start = (bf16[8,128,32,64]{1,3,2,0:T(8,128)(2,1)S(1)}, bf16[8,128,32,64]{1,3,2,0:T(8,128)(2,1)}, u32[]{:S(2)}) copy-start(bf16[8,128,32,64]{1,3,2,0:T(8,128)(2,1)} %copy.40) | copy-start | bytes 12582916
Sparse Core Ops, SparseCore 0:
  66.3 168.0 all-gather.3
  394.7 163.5 all-gather.5
